TPU v7x, 32 devices: a whole 2x2x4 slice. The times are simulated.
32 devices in a mesh: tm: 8 (over z, x), space: 4 (over y, core).
Axes of the slice: x: 2, y: 2, z: 4, core: 2. Of those that a mesh axis runs over, the one named last changes fastest.
Arguments:
- states: float32 [8, 2, 64, 256], P('tm', None, 'space'), may hold values from -6 to 6
- vel_x: int32 [64, 256], replicated, may hold values from -15 to 15
- vel_y: int32 [64, 256], replicated, may hold values from -15 to 15
- diffus: int32 [64, 256], replicated, may hold values from 1 to 10
Outputs:
- corrected: float32 [8, 2, 64, 256], P('tm', None, 'space')
- advanced: float32 [8, 2, 64, 256], P('tm', None, 'space')
- residual: float32 [8, 2, 64, 256], P('tm', None, 'space')
All inputs are finite; a program needn't handle non-finite values.
Results may differ from a plain program's by a relative error of at most 0.00002.
Values sent between devices are 32-bit elements; how exact they have to be, the bound alone decides.
A program may use at most 64 MiB of HBM per device.

v0:
```python
import jax
import jax.numpy as jnp
from jax import lax
from jax.sharding import PartitionSpec as P

STEPS = 16


def extended_2(block, sides, width):
    for axis, dim in sides:
        count = lax.axis_size(axis)
        forward = [(i, i + 1) for i in range(count - 1)]
        backward = [(target, source) for source, target in forward]
        low = lax.ppermute(
            lax.slice_in_dim(block, block.shape[dim] - width, None, axis=dim), axis, forward
        )
        high = lax.ppermute(lax.slice_in_dim(block, 0, width, axis=dim), axis, backward)
        block = jnp.concatenate([low, block, high], axis=dim)
    return block


def from_behind(value, axis, steps):
    count = lax.axis_size(axis)
    initial, last = (max(0, -steps), min(count, count - steps))
    return lax.ppermute(value, axis, [(source, source + steps) for source in range(initial, last)])


def tracer_scales():
    return jnp.array([1.0, 0.5], jnp.float32)[:, None, None]


def coefficients(vel_x, vel_y, diffus):
    return (
        0.01 * vel_x.astype(jnp.float32),
        0.01 * vel_y.astype(jnp.float32),
        0.005 * diffus.astype(jnp.float32),
    )


def advance(field, coefs, factor):
    courant_x, courant_y, diffusion = coefs
    padded = jnp.pad(field, ((0, 0), (1, 1), (1, 1)))
    row_above = padded[:, :-2, 1:-1]
    row_below = padded[:, 2:, 1:-1]
    column_left = padded[:, 1:-1, :-2]
    column_right = padded[:, 1:-1, 2:]
    transport = (
        jnp.maximum(courant_x, 0.0) * (field - row_above)
        + jnp.minimum(courant_x, 0.0) * (row_below - field)
        + jnp.maximum(courant_y, 0.0) * (field - column_left)
        + jnp.minimum(courant_y, 0.0) * (column_right - field)
    )
    laplace = row_above + row_below + column_left + column_right - 4.0 * field
    return field + factor * (diffusion * tracer_scales() * laplace - transport)


def on_device(states, vel_x, vel_y, diffus):
    row_count = states.shape[2]
    fine_reach = 4
    coarse_reach = 8
    grid_rows = vel_x.shape[0]
    tile_index = lax.axis_index("space")
    full_coefs = coefficients(vel_x, vel_y, diffus)

    def window(coefficient_table, reach):
        padded = jnp.pad(coefficient_table, ((reach, reach), (0, 0)))
        return lax.dynamic_slice_in_dim(padded, tile_index * row_count, row_count + 2 * reach, 0)

    def inside_mask(reach):
        global_row = tile_index * row_count - reach + lax.iota(jnp.int32, row_count + 2 * reach)
        return ((global_row >= 0) & (global_row < grid_rows)).astype(jnp.float32)[:, None]

    fine_coefs = tuple((window(table, fine_reach) for table in full_coefs))
    fine_inside = inside_mask(fine_reach)
    coarse_coefs = tuple((window(table, coarse_reach) for table in full_coefs))
    coarse_inside = inside_mask(coarse_reach)

    def fine_steps(field):
        for block_index in range(STEPS // fine_reach):
            extended = extended_2(field, (("space", 1),), fine_reach)
            for inner_index in range(fine_reach):
                extended = advance(extended, fine_coefs, 1.0) * fine_inside
            field = extended[:, fine_reach : fine_reach + row_count]
        return field

    def coarse_block(block_index, current):
        extended = extended_2(current, (("space", 1),), coarse_reach)
        for inner_index in range(coarse_reach):
            extended = advance(extended, coarse_coefs, 2.0) * coarse_inside
        return extended[:, coarse_reach : coarse_reach + row_count]

    def coarse_steps(field, count):
        return lax.fori_loop(0, count // coarse_reach, coarse_block, field)

    initial = states[0]
    first_slot = lax.axis_index("tm") == 0
    interval_ends = fine_steps(initial)
    received = from_behind(interval_ends, "tm", 1)
    starts = jnp.where(first_slot, initial, received)
    second_ends = fine_steps(starts)
    coarse_starts = coarse_steps(starts, STEPS // 2)
    received_second, received_coarse = from_behind((second_ends, coarse_starts), "tm", 1)
    residual = jnp.where(first_slot, jnp.zeros_like(starts), received_second - starts)
    forcing = jnp.where(first_slot, initial, received_second - received_coarse)
    corrected = forcing
    for section_bit in range(lax.axis_size("tm").bit_length() - 1):
        distant = from_behind(corrected, "tm", 1 << section_bit)
        distant = coarse_steps(distant, (1 << section_bit) * (STEPS // 2))
        corrected = corrected + distant
    advanced = fine_steps(corrected)
    return (corrected[None], advanced[None], residual[None])


def solution(mesh):
    return jax.shard_map(
        on_device,
        mesh=mesh,
        in_specs=(P("tm", None, "space", None), P(), P(), P()),
        out_specs=(
            P("tm", None, "space", None),
            P("tm", None, "space", None),
            P("tm", None, "space", None),
        ),
        check_vma=False,
    )
```

profile of v0, /device:TPU:19, one launch (start us, length us, event | category | flops | bytes accessed | tf_op | source)
XLA Modules:
  0.0 189.6 jit_solution(5812528330155849198)
XLA Ops:
  1.4 3.7 %collective-permute-start.4 = (f32[2,4,256]{2,1,0:T(4,128)S(1)}, f32[2,4,256]{2,1,0:T(4,128)S(1)}, u32[]{:S(2)}, u32[]{:S(2)}) collective-permute-start(f32[2,4,256]{2,1,0:T(4,128)S(1)} %get-tuple-element.687), channel_id=1, source_target_pairs={{0,1},{1,2},{2,3},{4,5},{5,6},{6,7},{8,9},{9,10},{10,11},{12,13},{... | collective-permute-start | bytes 24584 | tf_op jit(solution)/shard_map/ppermute | solution.py:14
  11.2 3.1 %collective-permute-start.6 = (f32[2,4,256]{2,1,0:T(4,128)S(1)}, f32[2,4,256]{2,1,0:T(4,128)S(1)}, u32[]{:S(2)}, u32[]{:S(2)}) collective-permute-start(f32[2,4,256]{2,1,0:T(4,128)S(1)} %get-tuple-element.674), channel_id=1, source_target_pairs={{0,1},{1,2},{2,3},{4,5},{5,6},{6,7},{8,9},{9,10},{10,11},{12,13},{... | collective-permute-start | bytes 24584 | tf_op jit(solution)/shard_map/ppermute | solution.py:14
  16.3 3.0 %collective-permute-done.7 = f32[2,4,256]{2,1,0:T(4,128)S(1)} collective-permute-done((f32[2,4,256]{2,1,0:T(4,128)S(1)}, f32[2,4,256]{2,1,0:T(4,128)S(1)}, u32[]{:S(2)}, u32[]{:S(2)}) %collective-permute-start.7) | collective-permute-done | bytes 8224 | tf_op jit(solution)/shard_map/ppermute | solution.py:17
  34.7 3.2 %collective-permute-start.12 = (f32[2,16,256]{2,1,0:T(8,128)S(1)}, f32[2,16,256]{2,1,0:T(8,128)S(1)}, u32[]{:S(2)}, u32[]{:S(2)}) collective-permute-start(f32[2,16,256]{2,1,0:T(8,128)S(1)} %fusion.296), channel_id=1, source_target_pairs={{0,4},{4,8},{8,12},{12,16},{16,20},{20,24},{24,28},{1,5},{5,9},{9,... | collective-permute-start | bytes 98312 | tf_op jit(solution)/shard_map/ppermute | solution.py:25
  39.3 3.1 %collective-permute-start.13 = (f32[2,4,256]{2,1,0:T(4,128)S(1)}, f32[2,4,256]{2,1,0:T(4,128)S(1)}, u32[]{:S(2)}, u32[]{:S(2)}) collective-permute-start(f32[2,4,256]{2,1,0:T(4,128)S(1)} %get-tuple-element.685), channel_id=1, source_target_pairs={{0,1},{1,2},{2,3},{4,5},{5,6},{6,7},{8,9},{9,10},{10,11},{12,13},{... | collective-permute-start | bytes 24584 | tf_op jit(solution)/shard_map/ppermute | solution.py:14
  44.5 2.9 %collective-permute-done.14 = f32[2,4,256]{2,1,0:T(4,128)S(1)} collective-permute-done((f32[2,4,256]{2,1,0:T(4,128)S(1)}, f32[2,4,256]{2,1,0:T(4,128)S(1)}, u32[]{:S(2)}, u32[]{:S(2)}) %collective-permute-start.14) | collective-permute-done | bytes 8224 | tf_op jit(solution)/shard_map/ppermute | solution.py:17
  52.2 3.2 %collective-permute-start.22 = (f32[2,8,256]{2,1,0:T(8,128)S(1)}, f32[2,8,256]{2,1,0:T(8,128)S(1)}, u32[]{:S(2)}, u32[]{:S(2)}) collective-permute-start(f32[2,8,256]{2,1,0:T(8,128)S(1)} %get-tuple-element.683), channel_id=1, source_target_pairs={{0,1},{1,2},{2,3},{4,5},{5,6},{6,7},{8,9},{9,10},{10,11},{12,13},{... | collective-permute-start | bytes 49160 | tf_op jit(solution)/shard_map/while/body/eval_jaxpr/ppermute | solution.py:14
  57.9 3.6 %collective-permute-start.17 = (f32[2,4,256]{2,1,0:T(4,128)S(1)}, f32[2,4,256]{2,1,0:T(4,128)S(1)}, u32[]{:S(2)}, u32[]{:S(2)}) collective-permute-start(f32[2,4,256]{2,1,0:T(4,128)S(1)} %get-tuple-element.661), channel_id=1, source_target_pairs={{0,1},{1,2},{2,3},{4,5},{5,6},{6,7},{8,9},{9,10},{10,11},{12,13},{... | collective-permute-start | bytes 24584 | tf_op jit(solution)/shard_map/ppermute | solution.py:14
  71.4 4.1 %collective-permute-start.24 = (f32[2,16,256]{2,1,0:T(8,128)S(1)}, f32[2,16,256]{2,1,0:T(8,128)S(1)}, u32[]{:S(2)}, u32[]{:S(2)}) collective-permute-start(f32[2,16,256]{2,1,0:T(8,128)S(1)} %fusion.280), channel_id=1, source_target_pairs={{0,4},{4,8},{8,12},{12,16},{16,20},{20,24},{24,28},{1,5},{5,9},{9,... | collective-permute-start | bytes 98312 | tf_op jit(solution)/shard_map/ppermute | solution.py:25
  78.6 2.7 %collective-permute-done.21 = f32[2,16,256]{2,1,0:T(8,128)S(1)} collective-permute-done((f32[2,16,256]{2,1,0:T(8,128)S(1)}, f32[2,16,256]{2,1,0:T(8,128)S(1)}, u32[]{:S(2)}, u32[]{:S(2)}) %collective-permute-start.21) | collective-permute-done | bytes 32800 | tf_op jit(solution)/shard_map/ppermute | solution.py:25
  81.9 3.2 %collective-permute-start.25 = (f32[2,16,256]{2,1,0:T(8,128)S(1)}, f32[2,16,256]{2,1,0:T(8,128)S(1)}, u32[]{:S(2)}, u32[]{:S(2)}) collective-permute-start(f32[2,16,256]{2,1,0:T(8,128)S(1)} %get-tuple-element.678), channel_id=1, source_target_pairs={{0,4},{4,8},{8,12},{12,16},{16,20},{20,24},{24,28},{1,5},{5,9},{9,... | collective-permute-start | bytes 98312 | tf_op jit(solution)/shard_map/ppermute | solution.py:25
  86.5 5.2 %collective-permute-start.26 = (f32[2,8,256]{2,1,0:T(8,128)S(1)}, f32[2,8,256]{2,1,0:T(8,128)S(1)}, u32[]{:S(2)}, u32[]{:S(2)}) collective-permute-start(f32[2,8,256]{2,1,0:T(8,128)S(1)} %get-tuple-element.682), channel_id=1, source_target_pairs={{0,1},{1,2},{2,3},{4,5},{5,6},{6,7},{8,9},{9,10},{10,11},{12,13},{... | collective-permute-start | bytes 49160 | tf_op jit(solution)/shard_map/while/body/eval_jaxpr/ppermute | solution.py:14
  93.7 3.1 %collective-permute-done.27 = f32[2,8,256]{2,1,0:T(8,128)S(1)} collective-permute-done((f32[2,8,256]{2,1,0:T(8,128)S(1)}, f32[2,8,256]{2,1,0:T(8,128)S(1)}, u32[]{:S(2)}, u32[]{:S(2)}) %collective-permute-start.27) | collective-permute-done | bytes 16416 | tf_op jit(solution)/shard_map/while/body/eval_jaxpr/ppermute | solution.py:17
  100.0 2.7 %collective-permute-done.28 = f32[2,16,256]{2,1,0:T(8,128)S(1)} collective-permute-done((f32[2,16,256]{2,1,0:T(8,128)S(1)}, f32[2,16,256]{2,1,0:T(8,128)S(1)}, u32[]{:S(2)}, u32[]{:S(2)}) %collective-permute-start.28) | collective-permute-done | bytes 32800 | tf_op jit(solution)/shard_map/ppermute | solution.py:25
  102.7 17.4 %while.38 = (s32[]{:T(128)}, f32[2,16,256]{2,1,0:T(8,128)S(1)}, f32[32,256]{1,0:T(8,128)S(1)}, f32[32,256]{1,0:T(8,128)S(1)}, f32[32,256]{1,0:T(8,128)S(1)}, /*index=5*/s32[]{:T(128)}, s32[]{:T(128)}, f32[2]{0:T(128)S(1)}) while((s32[]{:T(128)}, f32[2,16,256]{2,1,0:T(8,128)S(1)}, ...), condition=%wide.region_1.2_spmd.clone.clone.clone, body=%wide.region_0.1_spmd.sunk.clone.clone.clone.sunk | while | flops 2826402 | bytes 3458465 | solution.py:93
  102.7 3.1 %collective-permute-start = (f32[2,8,256]{2,1,0:T(8,128)S(1)}, f32[2,8,256]{2,1,0:T(8,128)S(1)}, u32[]{:S(2)}, u32[]{:S(2)}) collective-permute-start(f32[2,8,256]{2,1,0:T(8,128)S(1)} %get-tuple-element.787), channel_id=1, source_target_pairs={{0,1},{1,2},{2,3},{4,5},{5,6},{6,7},{8,9},{9,10},{10,11},{12,13},{... | collective-permute-start | bytes 49160 | tf_op jit(solution)/shard_map/while/body/eval_jaxpr/ppermute | solution.py:14
  107.9 3.0 %collective-permute-done.1 = f32[2,8,256]{2,1,0:T(8,128)S(1)} collective-permute-done((f32[2,8,256]{2,1,0:T(8,128)S(1)}, f32[2,8,256]{2,1,0:T(8,128)S(1)}, u32[]{:S(2)}, u32[]{:S(2)}) %collective-permute-start.1) | collective-permute-done | bytes 16416 | tf_op jit(solution)/shard_map/while/body/eval_jaxpr/ppermute | solution.py:17
  121.4 4.3 %collective-permute-done.29 = f32[2,16,256]{2,1,0:T(8,128)S(1)} collective-permute-done((f32[2,16,256]{2,1,0:T(8,128)S(1)}, f32[2,16,256]{2,1,0:T(8,128)S(1)}, u32[]{:S(2)}, u32[]{:S(2)}) %collective-permute-start.29) | collective-permute-done | bytes 32800 | tf_op jit(solution)/shard_map/ppermute | solution.py:25
  125.7 33.6 %while.39 = (s32[]{:T(128)}, f32[2,16,256]{2,1,0:T(8,128)S(1)}, f32[32,256]{1,0:T(8,128)S(1)}, f32[32,256]{1,0:T(8,128)S(1)}, f32[32,256]{1,0:T(8,128)S(1)}, /*index=5*/s32[]{:T(128)}, s32[]{:T(128)}, f32[2]{0:T(128)S(1)}) while((s32[]{:T(128)}, f32[2,16,256]{2,1,0:T(8,128)S(1)}, ...), condition=%wide.region_3.4_spmd.clone.clone.clone, body=%wide.region_2.3_spmd.sunk.clone.clone.clone.sunk | while | flops 2826402 | bytes 3458465 | solution.py:93
  125.7 3.1 %collective-permute-start.2 = (f32[2,8,256]{2,1,0:T(8,128)S(1)}, f32[2,8,256]{2,1,0:T(8,128)S(1)}, u32[]{:S(2)}, u32[]{:S(2)}) collective-permute-start(f32[2,8,256]{2,1,0:T(8,128)S(1)} %get-tuple-element.806), channel_id=1, source_target_pairs={{0,1},{1,2},{2,3},{4,5},{5,6},{6,7},{8,9},{9,10},{10,11},{12,13},{... | collective-permute-start | bytes 49160 | tf_op jit(solution)/shard_map/while/body/eval_jaxpr/ppermute | solution.py:14
  130.8 3.0 %collective-permute-done.3 = f32[2,8,256]{2,1,0:T(8,128)S(1)} collective-permute-done((f32[2,8,256]{2,1,0:T(8,128)S(1)}, f32[2,8,256]{2,1,0:T(8,128)S(1)}, u32[]{:S(2)}, u32[]{:S(2)}) %collective-permute-start.3) | collective-permute-done | bytes 16416 | tf_op jit(solution)/shard_map/while/body/eval_jaxpr/ppermute | solution.py:17
  163.6 2.6 %collective-permute-done.31 = f32[2,4,256]{2,1,0:T(4,128)S(1)} collective-permute-done((f32[2,4,256]{2,1,0:T(4,128)S(1)}, f32[2,4,256]{2,1,0:T(4,128)S(1)}, u32[]{:S(2)}, u32[]{:S(2)}) %collective-permute-start.31) | collective-permute-done | bytes 8224 | tf_op jit(solution)/shard_map/ppermute | solution.py:17
  178.5 2.6 %collective-permute-done.35 = f32[2,4,256]{2,1,0:T(4,128)S(1)} collective-permute-done((f32[2,4,256]{2,1,0:T(4,128)S(1)}, f32[2,4,256]{2,1,0:T(4,128)S(1)}, u32[]{:S(2)}, u32[]{:S(2)}) %collective-permute-start.35) | collective-permute-done | bytes 8224 | tf_op jit(solution)/shard_map/ppermute | solution.py:17
  185.9 2.6 %collective-permute-done.37 = f32[2,4,256]{2,1,0:T(4,128)S(1)} collective-permute-done((f32[2,4,256]{2,1,0:T(4,128)S(1)}, f32[2,4,256]{2,1,0:T(4,128)S(1)}, u32[]{:S(2)}, u32[]{:S(2)}) %collective-permute-start.37) | collective-permute-done | bytes 8224 | tf_op jit(solution)/shard_map/ppermute | solution.py:17
  (314 shorter events, 116.0 us)
Async XLA Ops:
  1.4 7.5 %collective-permute-start.4 = (f32[2,4,256]{2,1,0:T(4,128)S(1)}, f32[2,4,256]{2,1,0:T(4,128)S(1)}, u32[]{:S(2)}, u32[]{:S(2)}) collective-permute-start(f32[2,4,256]{2,1,0:T(4,128)S(1)} %get-tuple-element.687), channel_id=1, source_target_pairs={{0,1},{1,2},{2,3},{4,5},{5,6},{6,7},{8,9},{9,10},{10,11},{12,13},{... | collective-permute-start | bytes 24584 | tf_op jit(solution)/shard_map/ppermute | solution.py:14
  5.1 5.0 %collective-permute-start.5 = (f32[2,4,256]{2,1,0:T(4,128)S(1)}, f32[2,4,256]{2,1,0:T(4,128)S(1)}, u32[]{:S(2)}, u32[]{:S(2)}) collective-permute-start(f32[2,4,256]{2,1,0:T(4,128)S(1)} %get-tuple-element.688), channel_id=1, source_target_pairs={{1,0},{2,1},{3,2},{5,4},{6,5},{7,6},{9,8},{10,9},{11,10},{13,12},{... | collective-permute-start | bytes 24584 | tf_op jit(solution)/shard_map/ppermute | solution.py:17
  11.2 5.1 %collective-permute-start.6 = (f32[2,4,256]{2,1,0:T(4,128)S(1)}, f32[2,4,256]{2,1,0:T(4,128)S(1)}, u32[]{:S(2)}, u32[]{:S(2)}) collective-permute-start(f32[2,4,256]{2,1,0:T(4,128)S(1)} %get-tuple-element.674), channel_id=1, source_target_pairs={{0,1},{1,2},{2,3},{4,5},{5,6},{6,7},{8,9},{9,10},{10,11},{12,13},{... | collective-permute-start | bytes 24584 | tf_op jit(solution)/shard_map/ppermute | solution.py:14
  39.3 5.1 %collective-permute-start.13 = (f32[2,4,256]{2,1,0:T(4,128)S(1)}, f32[2,4,256]{2,1,0:T(4,128)S(1)}, u32[]{:S(2)}, u32[]{:S(2)}) collective-permute-start(f32[2,4,256]{2,1,0:T(4,128)S(1)} %get-tuple-element.685), channel_id=1, source_target_pairs={{0,1},{1,2},{2,3},{4,5},{5,6},{6,7},{8,9},{9,10},{10,11},{12,13},{... | collective-permute-start | bytes 24584 | tf_op jit(solution)/shard_map/ppermute | solution.py:14
  47.9 9.5 %collective-permute-start.15 = (f32[2,4,256]{2,1,0:T(4,128)S(1)}, f32[2,4,256]{2,1,0:T(4,128)S(1)}, u32[]{:S(2)}, u32[]{:S(2)}) collective-permute-start(f32[2,4,256]{2,1,0:T(4,128)S(1)} %get-tuple-element.663), channel_id=1, source_target_pairs={{0,1},{1,2},{2,3},{4,5},{5,6},{6,7},{8,9},{9,10},{10,11},{12,13},{... | collective-permute-start | bytes 24584 | tf_op jit(solution)/shard_map/ppermute | solution.py:14
  49.8 7.5 %collective-permute-start.16 = (f32[2,4,256]{2,1,0:T(4,128)S(1)}, f32[2,4,256]{2,1,0:T(4,128)S(1)}, u32[]{:S(2)}, u32[]{:S(2)}) collective-permute-start(f32[2,4,256]{2,1,0:T(4,128)S(1)} %get-tuple-element.664), channel_id=1, source_target_pairs={{1,0},{2,1},{3,2},{5,4},{6,5},{7,6},{9,8},{10,9},{11,10},{13,12},{... | collective-permute-start | bytes 24584 | tf_op jit(solution)/shard_map/ppermute | solution.py:17
  52.2 11.2 %collective-permute-start.22 = (f32[2,8,256]{2,1,0:T(8,128)S(1)}, f32[2,8,256]{2,1,0:T(8,128)S(1)}, u32[]{:S(2)}, u32[]{:S(2)}) collective-permute-start(f32[2,8,256]{2,1,0:T(8,128)S(1)} %get-tuple-element.683), channel_id=1, source_target_pairs={{0,1},{1,2},{2,3},{4,5},{5,6},{6,7},{8,9},{9,10},{10,11},{12,13},{... | collective-permute-start | bytes 49160 | tf_op jit(solution)/shard_map/while/body/eval_jaxpr/ppermute | solution.py:14
  55.4 8.1 %collective-permute-start.23 = (f32[2,8,256]{2,1,0:T(8,128)S(1)}, f32[2,8,256]{2,1,0:T(8,128)S(1)}, u32[]{:S(2)}, u32[]{:S(2)}) collective-permute-start(f32[2,8,256]{2,1,0:T(8,128)S(1)} %get-tuple-element.684), channel_id=1, source_target_pairs={{1,0},{2,1},{3,2},{5,4},{6,5},{7,6},{9,8},{10,9},{11,10},{13,12},{... | collective-permute-start | bytes 49160 | tf_op jit(solution)/shard_map/while/body/eval_jaxpr/ppermute | solution.py:17
  57.9 6.7 %collective-permute-start.17 = (f32[2,4,256]{2,1,0:T(4,128)S(1)}, f32[2,4,256]{2,1,0:T(4,128)S(1)}, u32[]{:S(2)}, u32[]{:S(2)}) collective-permute-start(f32[2,4,256]{2,1,0:T(4,128)S(1)} %get-tuple-element.661), channel_id=1, source_target_pairs={{0,1},{1,2},{2,3},{4,5},{5,6},{6,7},{8,9},{9,10},{10,11},{12,13},{... | collective-permute-start | bytes 24584 | tf_op jit(solution)/shard_map/ppermute | solution.py:14
  67.0 8.5 %collective-permute-start.19 = (f32[2,4,256]{2,1,0:T(4,128)S(1)}, f32[2,4,256]{2,1,0:T(4,128)S(1)}, u32[]{:S(2)}, u32[]{:S(2)}) collective-permute-start(f32[2,4,256]{2,1,0:T(4,128)S(1)} %get-tuple-element.659), channel_id=1, source_target_pairs={{0,1},{1,2},{2,3},{4,5},{5,6},{6,7},{8,9},{9,10},{10,11},{12,13},{... | collective-permute-start | bytes 24584 | tf_op jit(solution)/shard_map/ppermute | solution.py:14
  69.0 6.6 %collective-permute-start.20 = (f32[2,4,256]{2,1,0:T(4,128)S(1)}, f32[2,4,256]{2,1,0:T(4,128)S(1)}, u32[]{:S(2)}, u32[]{:S(2)}) collective-permute-start(f32[2,4,256]{2,1,0:T(4,128)S(1)} %get-tuple-element.660), channel_id=1, source_target_pairs={{1,0},{2,1},{3,2},{5,4},{6,5},{7,6},{9,8},{10,9},{11,10},{13,12},{... | collective-permute-start | bytes 24584 | tf_op jit(solution)/shard_map/ppermute | solution.py:17
  71.4 7.1 %collective-permute-start.24 = (f32[2,16,256]{2,1,0:T(8,128)S(1)}, f32[2,16,256]{2,1,0:T(8,128)S(1)}, u32[]{:S(2)}, u32[]{:S(2)}) collective-permute-start(f32[2,16,256]{2,1,0:T(8,128)S(1)} %fusion.280), channel_id=1, source_target_pairs={{0,4},{4,8},{8,12},{12,16},{16,20},{20,24},{24,28},{1,5},{5,9},{9,... | collective-permute-start | bytes 98312 | tf_op jit(solution)/shard_map/ppermute | solution.py:25
  76.1 5.2 %collective-permute-start.21 = (f32[2,16,256]{2,1,0:T(8,128)S(1)}, f32[2,16,256]{2,1,0:T(8,128)S(1)}, u32[]{:S(2)}, u32[]{:S(2)}) collective-permute-start(f32[2,16,256]{2,1,0:T(8,128)S(1)} %fusion.289), channel_id=1, source_target_pairs={{0,4},{4,8},{8,12},{12,16},{16,20},{20,24},{24,28},{1,5},{5,9},{9,... | collective-permute-start | bytes 98312 | tf_op jit(solution)/shard_map/ppermute | solution.py:25
  86.5 7.2 %collective-permute-start.26 = (f32[2,8,256]{2,1,0:T(8,128)S(1)}, f32[2,8,256]{2,1,0:T(8,128)S(1)}, u32[]{:S(2)}, u32[]{:S(2)}) collective-permute-start(f32[2,8,256]{2,1,0:T(8,128)S(1)} %get-tuple-element.682), channel_id=1, source_target_pairs={{0,1},{1,2},{2,3},{4,5},{5,6},{6,7},{8,9},{9,10},{10,11},{12,13},{... | collective-permute-start | bytes 49160 | tf_op jit(solution)/shard_map/while/body/eval_jaxpr/ppermute | solution.py:14
  91.8 5.1 %collective-permute-start.27 = (f32[2,8,256]{2,1,0:T(8,128)S(1)}, f32[2,8,256]{2,1,0:T(8,128)S(1)}, u32[]{:S(2)}, u32[]{:S(2)}) collective-permute-start(f32[2,8,256]{2,1,0:T(8,128)S(1)} %get-tuple-element.681), channel_id=1, source_target_pairs={{1,0},{2,1},{3,2},{5,4},{6,5},{7,6},{9,8},{10,9},{11,10},{13,12},{... | collective-permute-start | bytes 49160 | tf_op jit(solution)/shard_map/while/body/eval_jaxpr/ppermute | solution.py:17
  102.7 5.1 %collective-permute-start = (f32[2,8,256]{2,1,0:T(8,128)S(1)}, f32[2,8,256]{2,1,0:T(8,128)S(1)}, u32[]{:S(2)}, u32[]{:S(2)}) collective-permute-start(f32[2,8,256]{2,1,0:T(8,128)S(1)} %get-tuple-element.787), channel_id=1, source_target_pairs={{0,1},{1,2},{2,3},{4,5},{5,6},{6,7},{8,9},{9,10},{10,11},{12,13},{... | collective-permute-start | bytes 49160 | tf_op jit(solution)/shard_map/while/body/eval_jaxpr/ppermute | solution.py:14
  105.8 5.1 %collective-permute-start.1 = (f32[2,8,256]{2,1,0:T(8,128)S(1)}, f32[2,8,256]{2,1,0:T(8,128)S(1)}, u32[]{:S(2)}, u32[]{:S(2)}) collective-permute-start(f32[2,8,256]{2,1,0:T(8,128)S(1)} %get-tuple-element.788), channel_id=1, source_target_pairs={{1,0},{2,1},{3,2},{5,4},{6,5},{7,6},{9,8},{10,9},{11,10},{13,12},{... | collective-permute-start | bytes 49160 | tf_op jit(solution)/shard_map/while/body/eval_jaxpr/ppermute | solution.py:17
  113.9 5.1 %collective-permute-start.1 = (f32[2,8,256]{2,1,0:T(8,128)S(1)}, f32[2,8,256]{2,1,0:T(8,128)S(1)}, u32[]{:S(2)}, u32[]{:S(2)}) collective-permute-start(f32[2,8,256]{2,1,0:T(8,128)S(1)} %get-tuple-element.788), channel_id=1, source_target_pairs={{1,0},{2,1},{3,2},{5,4},{6,5},{7,6},{9,8},{10,9},{11,10},{13,12},{... | collective-permute-start | bytes 49160 | tf_op jit(solution)/shard_map/while/body/eval_jaxpr/ppermute | solution.py:17
  120.1 5.6 %collective-permute-start.29 = (f32[2,16,256]{2,1,0:T(8,128)S(1)}, f32[2,16,256]{2,1,0:T(8,128)S(1)}, u32[]{:S(2)}, u32[]{:S(2)}) collective-permute-start(f32[2,16,256]{2,1,0:T(8,128)S(1)} %add.2700), channel_id=1, source_target_pairs={{0,16},{4,20},{8,24},{12,28},{1,17},{5,21},{9,25},{13,29},{2,18},{... | collective-permute-start | bytes 98312 | tf_op jit(solution)/shard_map/ppermute | solution.py:25
  125.7 5.1 %collective-permute-start.2 = (f32[2,8,256]{2,1,0:T(8,128)S(1)}, f32[2,8,256]{2,1,0:T(8,128)S(1)}, u32[]{:S(2)}, u32[]{:S(2)}) collective-permute-start(f32[2,8,256]{2,1,0:T(8,128)S(1)} %get-tuple-element.806), channel_id=1, source_target_pairs={{0,1},{1,2},{2,3},{4,5},{5,6},{6,7},{8,9},{9,10},{10,11},{12,13},{... | collective-permute-start | bytes 49160 | tf_op jit(solution)/shard_map/while/body/eval_jaxpr/ppermute | solution.py:14
  128.8 5.1 %collective-permute-start.3 = (f32[2,8,256]{2,1,0:T(8,128)S(1)}, f32[2,8,256]{2,1,0:T(8,128)S(1)}, u32[]{:S(2)}, u32[]{:S(2)}) collective-permute-start(f32[2,8,256]{2,1,0:T(8,128)S(1)} %get-tuple-element.807), channel_id=1, source_target_pairs={{1,0},{2,1},{3,2},{5,4},{6,5},{7,6},{9,8},{10,9},{11,10},{13,12},{... | collective-permute-start | bytes 49160 | tf_op jit(solution)/shard_map/while/body/eval_jaxpr/ppermute | solution.py:17
  136.9 5.1 %collective-permute-start.3 = (f32[2,8,256]{2,1,0:T(8,128)S(1)}, f32[2,8,256]{2,1,0:T(8,128)S(1)}, u32[]{:S(2)}, u32[]{:S(2)}) collective-permute-start(f32[2,8,256]{2,1,0:T(8,128)S(1)} %get-tuple-element.807), channel_id=1, source_target_pairs={{1,0},{2,1},{3,2},{5,4},{6,5},{7,6},{9,8},{10,9},{11,10},{13,12},{... | collective-permute-start | bytes 49160 | tf_op jit(solution)/shard_map/while/body/eval_jaxpr/ppermute | solution.py:17
  145.0 5.1 %collective-permute-start.3 = (f32[2,8,256]{2,1,0:T(8,128)S(1)}, f32[2,8,256]{2,1,0:T(8,128)S(1)}, u32[]{:S(2)}, u32[]{:S(2)}) collective-permute-start(f32[2,8,256]{2,1,0:T(8,128)S(1)} %get-tuple-element.807), channel_id=1, source_target_pairs={{1,0},{2,1},{3,2},{5,4},{6,5},{7,6},{9,8},{10,9},{11,10},{13,12},{... | collective-permute-start | bytes 49160 | tf_op jit(solution)/shard_map/while/body/eval_jaxpr/ppermute | solution.py:17
  153.1 5.1 %collective-permute-start.3 = (f32[2,8,256]{2,1,0:T(8,128)S(1)}, f32[2,8,256]{2,1,0:T(8,128)S(1)}, u32[]{:S(2)}, u32[]{:S(2)}) collective-permute-start(f32[2,8,256]{2,1,0:T(8,128)S(1)} %get-tuple-element.807), channel_id=1, source_target_pairs={{1,0},{2,1},{3,2},{5,4},{6,5},{7,6},{9,8},{10,9},{11,10},{13,12},{... | collective-permute-start | bytes 49160 | tf_op jit(solution)/shard_map/while/body/eval_jaxpr/ppermute | solution.py:17
  (29 other events, 123.8 us)
where the time goes:
time: 192 us; the launch traced here: 190 us
  starting transfers between devices  112 us (58%)
  waiting for transfers between devices  56.1 us (29%)
  other arithmetic  16.2 us (8%)
  local copies, waits for them, and re-layouts  3.07 us (2%)
  between operations  1.93 us (1%)
    ppermute x20, starting transfers between devices, extended_2(): lax.ppermute(lax.slice_in_dim(block, block.shape[dim] - width, None, axis...  51.4 us
    ppermute x20, starting transfers between devices, extended_2(): lax.ppermute(lax.slice_in_dim(block, 0, width, axis=dim), axis, backward)  44 us
    ppermute x20, waiting for transfers between devices, extended_2(): lax.ppermute(lax.slice_in_dim(block, 0, width, axis=dim), axis, backward)  43.5 us
    ppermute x6, starting transfers between devices, from_behind(): lax.ppermute(value, axis, [(source, source + steps) for source in range(i...  16.2 us
    ppermute x6, waiting for transfers between devices, from_behind(): lax.ppermute(value, axis, [(source, source + steps) for source in range(i...  12.5 us
    mul x55, other arithmetic, coarse_block(): extended = advance(extended, coarse_coefs, 2.0) * coarse_inside  6.26 us
    mul x46, other arithmetic, fine_steps(): extended = advance(extended, fine_coefs, 1.0) * fine_inside  4.81 us
  transfers between devices with their start and end apart: 46, of which 22 were waited for; matrix products, arithmetic and copies ran while one was open for 2% of the time, Pallas kernels for 0%

commit v1 on v0

v1 whole, which is shorter than its diff:
```python
import functools

import jax
import jax.numpy as jnp
from jax import lax
from jax.experimental import pallas as pl
from jax.experimental.pallas import tpu as pltpu
from jax.sharding import PartitionSpec as P

STEPS = 16
COARSE = STEPS // 2
LANES = 128
SUB = 8
MESH = pl.DeviceIdType.MESH


def load(ref, stacks, tiles):
    return [[ref[k, :, w * LANES : (w + 1) * LANES] for w in range(tiles)] for k in range(stacks)]


def load_rows(ref, stacks, tiles):
    return [[ref[w, pl.ds(k, SUB, stride=stacks), :] for w in range(tiles)] for k in range(stacks)]


def store(ref, u):
    for k, row in enumerate(u):
        for w, value in enumerate(row):
            ref[k, :, w * LANES : (w + 1) * LANES] = value


def store_rows(ref, u):
    stacks = len(u)
    for k, row in enumerate(u):
        for w, value in enumerate(row):
            ref[w, pl.ds(k, SUB, stride=stacks), :] = value


def each(f, *fields):
    return [[f(*values) for values in zip(*rows)] for rows in zip(*fields)]


def advance(fields, coefs):
    stacks, tiles = len(fields[0]), len(fields[0][0])
    lane = lax.broadcasted_iota(jnp.int32, (SUB, LANES), 1)
    first, last = lane == 0, lane == LANES - 1
    out = [[[None] * tiles for _ in range(stacks)] for _ in fields]
    tops = [[pltpu.roll(u[stacks - 1][w], 1, 0) for w in range(tiles)] for u in fields]
    bottoms = [[pltpu.roll(u[0][w], SUB - 1, 0) for w in range(tiles)] for u in fields]
    for k in range(stacks):
        c = [[coefs[i, k, :, w * LANES : (w + 1) * LANES] for w in range(tiles)] for i in range(5)]
        for f, u in enumerate(fields):
            right = [pltpu.roll(v, 1, 1) for v in u[k]]
            left = [pltpu.roll(v, LANES - 1, 1) for v in u[k]]
            for w in range(tiles):
                a = u[k - 1][w] if k else tops[f][w]
                b = u[k + 1][w] if k + 1 < stacks else bottoms[f][w]
                l = jnp.where(first, right[w - 1], right[w]) if w else right[w]
                r = jnp.where(last, left[w + 1], left[w]) if w + 1 < tiles else left[w]
                out[f][k][w] = (c[0][w] * u[k][w] + (c[1][w] * a + c[2][w] * b)) + (c[3][w] * l + c[4][w] * r)
    return out


def propagate(fields, coefs, count):
    return lax.fori_loop(0, count, lambda _, now: advance(now, coefs), fields)


def kernel(
    states, vel_x, vel_y, diffus, corrected, advanced, residual,
    tables, fine, coarse, gathered, starts, addends, last_residual, blocks, plain,
    table_sem, send_sem, recv_sem, block_send, block_recv, out_send, out_recv,
):
    groups, places = lax.axis_size("tm") // 2, lax.axis_size("space")
    p, s = lax.axis_index("tm"), lax.axis_index("space")
    g = lax.div(p, 2)
    x = p - 2 * g
    tracer = lax.rem(s, 2)
    partner = s + 1 - 2 * tracer
    rows = states.shape[2]
    stacks, tiles = fine.shape[1], fine.shape[3] // LANES

    def columns(w):
        return pl.ds(w * LANES, LANES)

    loads = [
        pltpu.make_async_copy(ref.at[:, columns(w)], tables.at[i, w], table_sem.at[i, w])
        for i, ref in enumerate((vel_x, vel_y, diffus))
        for w in range(tiles)
    ]
    for copy in loads:
        copy.start()

    barrier = pltpu.get_barrier_semaphore()

    def greet(pp, ss):
        pl.semaphore_signal(barrier, 1, device_id=(pp, ss), device_id_type=MESH)

    for ss in range(places):
        @pl.when((x == 1) | (s != ss))
        def _():
            greet(2 * g, ss)

        @pl.when(g > 0)
        def _():
            greet(2 * g - 2, ss)
            greet(2 * g - 1, ss)

    greet(p, partner)

    def greet_block(i, carry):
        greet(2 * i + x, s)
        return carry

    lax.fori_loop(0, g, greet_block, 0)
    ahead = groups - 1 - g
    more = jnp.where(ahead > 0, 2 * places, 0)
    pl.semaphore_wait(barrier, (1 - x) * (2 * places - 1) + more + ahead + 1)

    my_rows = pl.ds(pl.multiple_of(s * rows, SUB), rows)
    partner_rows = pl.ds(pl.multiple_of(partner * rows, SUB), rows)

    def piece(role, pp, ss, slot, w):
        return pltpu.make_async_remote_copy(
            src_ref=states.at[0, ss % 2, :, columns(w)],
            dst_ref=gathered.at[role, w, my_rows],
            send_sem=send_sem.at[slot, w],
            recv_sem=recv_sem.at[role],
            device_id=(pp, ss),
            device_id_type=MESH,
        )

    own = [
        pltpu.make_async_copy(states.at[0, tracer, :, columns(w)], gathered.at[2, w, my_rows], recv_sem.at[2])
        for w in range(tiles)
    ]

    def to_next(act):
        @pl.when(ahead > 0)
        def _():
            for m in range(2):
                for ss in range(places):
                    for w in range(tiles):
                        act(piece(x, 2 * g + 2 + m, ss, m * places + ss, w))

    def to_group(act):
        @pl.when(x == 0)
        def _():
            for ss in range(places):
                for w in range(tiles):
                    act(piece(2, 2 * g + 1, ss, 3 * places + ss, w))
            for ss in range(places):
                @pl.when(s != ss)
                def _():
                    for w in range(tiles):
                        act(piece(2, 2 * g, ss, 2 * places + ss, w))

    to_next(lambda copy: copy.start())
    to_group(lambda copy: copy.start())

    @pl.when(x == 0)
    def _():
        for copy in own:
            copy.start()

    @pl.when(g == 0)
    def _():
        gathered[0] = jnp.zeros(gathered.shape[1:], jnp.float32)
        gathered[1] = jnp.zeros(gathered.shape[1:], jnp.float32)

    for copy in loads:
        copy.wait()
    scale = jnp.where(tracer == 0, 1.0, 0.5).astype(jnp.float32)
    sub = lax.broadcasted_iota(jnp.int32, (SUB, LANES), 0)
    lane = lax.broadcasted_iota(jnp.int32, (SUB, LANES), 1)
    for k, w in [(k, w) for k in range(stacks) for w in range(tiles)]:
        cx, cy, d = (tables[i, w, pl.ds(k, SUB, stride=stacks), :].astype(jnp.float32) for i in range(3))
        cx, cy, d = 0.01 * cx, 0.01 * cy, (0.005 * d) * scale
        above, below = d + jnp.maximum(cx, 0.0), d - jnp.minimum(cx, 0.0)
        before, after = d + jnp.maximum(cy, 0.0), d - jnp.minimum(cy, 0.0)
        total = (above + below) + (before + after)
        if k == 0:
            above = jnp.where(sub == 0, 0.0, above)
        if k == stacks - 1:
            below = jnp.where(sub == SUB - 1, 0.0, below)
        if w == 0:
            before = jnp.where(lane == 0, 0.0, before)
        if w == tiles - 1:
            after = jnp.where(lane == LANES - 1, 0.0, after)
        for table, factor in ((fine, 1.0), (coarse, 2.0)):
            table[0, k, :, columns(w)] = 1.0 - factor * total
            for i, value in enumerate((above, below, before, after)):
                table[i + 1, k, :, columns(w)] = factor * value

    def arrive(role):
        pltpu.make_async_remote_copy(
            src_ref=gathered.at[role],
            dst_ref=gathered.at[role],
            send_sem=send_sem.at[0, 0],
            recv_sem=recv_sem.at[role],
            device_id=(p, partner),
            device_id_type=MESH,
        ).wait_recv()

    arrive(2)

    @pl.when(g > 0)
    def _():
        arrive(0)
        arrive(1)

    a0, b0, d0 = (load_rows(gathered.at[role], stacks, tiles) for role in range(3))
    a1, b1, d1 = propagate([a0, b0, d0], fine, STEPS)
    at_start = g == 0
    b1 = each(lambda u, v: jnp.where(at_start, v, u), b1, load_rows(gathered.at[2], stacks, tiles))
    store(starts.at[0], b1)
    store(starts.at[1], d1)
    a2, b2 = propagate([a1, b1], fine, STEPS)
    r0 = each(lambda u, v: jnp.where(at_start, 0.0, u - v), a2, load(starts.at[0], stacks, tiles))
    store(addends.at[0], r0)
    r1 = each(lambda u, v: u - v, b2, load(starts.at[1], stacks, tiles))
    store(last_residual, r1)
    (block,) = propagate([r0], coarse, COARSE)
    store(addends.at[1], each(lambda u, v: u + v, block, load(last_residual, stacks, tiles)))

    def block_copy(i):
        return pltpu.make_async_remote_copy(
            src_ref=addends.at[1],
            dst_ref=blocks.at[g],
            send_sem=block_send.at[i],
            recv_sem=block_recv.at[g],
            device_id=(2 * i + x, s),
            device_id_type=MESH,
        )

    def start_block(n, carry):
        block_copy(groups - 1 - n).start()
        return carry

    lax.fori_loop(0, ahead, start_block, 0)

    def hand_over(which, out, w):
        return pltpu.make_async_remote_copy(
            src_ref=plain.at[which, w, partner_rows],
            dst_ref=out.at[0, tracer, :, columns(w)],
            send_sem=out_send.at[which, w],
            recv_sem=out_recv.at[which, w],
            device_id=(p, partner),
            device_id_type=MESH,
        )

    def put(which, out, u):
        store_rows(plain.at[which], u)
        for w in range(tiles):
            hand_over(which, out, w).start()
        for w in range(tiles):
            out[0, tracer, :, columns(w)] = plain[which, w, my_rows]

    put(0, residual, each(lambda u, v: jnp.where(x == 0, u, v), load(addends.at[0], stacks, tiles), load(last_residual, stacks, tiles)))

    def take_block(i, e):
        (e,) = propagate([e], coarse, STEPS)
        pltpu.make_async_remote_copy(
            src_ref=addends.at[1],
            dst_ref=blocks.at[i],
            send_sem=block_send.at[0],
            recv_sem=block_recv.at[i],
            device_id=(p, partner),
            device_id_type=MESH,
        ).wait_recv()
        return each(lambda u, v: u + v, e, load(blocks.at[i], stacks, tiles))

    zero = [[jnp.zeros((SUB, LANES), jnp.float32)] * tiles for _ in range(stacks)]
    e = lax.fori_loop(0, g, take_block, zero)
    (e,) = propagate([e], coarse, COARSE * (1 + x))
    e = each(lambda u, v: u + v, e, load(addends.at[x], stacks, tiles))
    now = each(lambda u, v: u + v, e, load(starts.at[x], stacks, tiles))
    put(1, corrected, now)
    (now,) = propagate([now], fine, STEPS)
    put(2, advanced, now)

    to_next(lambda copy: copy.wait_send())
    to_group(lambda copy: copy.wait_send())

    def end_block(n, carry):
        block_copy(groups - 1 - n).wait_send()
        return carry

    lax.fori_loop(0, ahead, end_block, 0)
    for which, out in enumerate((residual, corrected, advanced)):
        for w in range(tiles):
            hand_over(which, out, w).wait()


def on_device(states, vel_x, vel_y, diffus):
    groups, places = lax.axis_size("tm") // 2, lax.axis_size("space")
    nx, cols = vel_x.shape
    stacks = nx // SUB
    tiles = cols // LANES
    field, grid = (stacks, SUB, cols), (tiles, nx, LANES)
    out = jax.ShapeDtypeStruct(states.shape, jnp.float32)
    return pl.pallas_call(
        kernel,
        out_shape=(out, out, out),
        in_specs=[pl.BlockSpec(memory_space=pl.ANY)] * 4,
        out_specs=(pl.BlockSpec(memory_space=pltpu.VMEM),) * 3,
        scratch_shapes=[
            pltpu.VMEM((3, *grid), jnp.int32),
            pltpu.VMEM((5, *field), jnp.float32),
            pltpu.VMEM((5, *field), jnp.float32),
            pltpu.VMEM((3, *grid), jnp.float32),
            pltpu.VMEM((2, *field), jnp.float32),
            pltpu.VMEM((2, *field), jnp.float32),
            pltpu.VMEM(field, jnp.float32),
            pltpu.VMEM((groups, *field), jnp.float32),
            pltpu.VMEM((3, *grid), jnp.float32),
            pltpu.SemaphoreType.DMA((3, tiles)),
            pltpu.SemaphoreType.DMA((4 * places, tiles)),
            pltpu.SemaphoreType.DMA((3,)),
            pltpu.SemaphoreType.DMA((groups,)),
            pltpu.SemaphoreType.DMA((groups,)),
            pltpu.SemaphoreType.DMA((3, tiles)),
            pltpu.SemaphoreType.DMA((3, tiles)),
        ],
        compiler_params=pltpu.CompilerParams(collective_id=0, has_side_effects=True),
    )(states, vel_x, vel_y, diffus)


def solution(mesh):
    split = P("tm", None, "space", None)
    return jax.shard_map(
        on_device,
        mesh=mesh,
        in_specs=(split, P(), P(), P()),
        out_specs=(split, split, split),
        check_vma=False,
    )
```

time: 192 us -> 29.9 us (0.16)
  starting transfers between devices: 112 us -> 0 us
  waiting for transfers between devices: 56.1 us -> 0 us
  Pallas kernels: 0 us -> 26 us
  other arithmetic: 16.2 us -> 0 us
    ppermute x46 -> x0, starting transfers between devices: 112 us -> none  [the longest x20 51.4 us: extended_2(): lax.ppermute(lax.slice_in_dim(block, block.shape[dim] - width, None, axis...]
    ppermute x46 -> x0, waiting for transfers between devices: 56.1 us -> none  [the longest x20 43.5 us: extended_2(): lax.ppermute(lax.slice_in_dim(block, 0, width, axis=dim), axis, backward)]
    pallas_call x0 -> x1, Pallas kernels: none -> 26 us  [on_device(): pl.pallas_call(kernel, out_shape=(out, out, out), in_specs=[pl.BlockSpec(...]
    mul x113 -> x0, other arithmetic: 13.1 us -> none  [the longest x55 6.26 us: coarse_block(): extended = advance(extended, coarse_coefs, 2.0) * coarse_inside]
  transfers between devices with their start and end apart: 46 -> 0, of which waited for: 22 -> 0; matrix products, arithmetic and copies ran while one was open for 2% -> 0% of each run, Pallas kernels for 0% -> 0%
where the time goes in v1:
time: 29.9 us; the launch traced here: 29.4 us
  Pallas kernels  26 us (87%)
  local copies, waits for them, and re-layouts  2.77 us (9%)
  between operations  0.65 us (2%)
    pallas_call x1, Pallas kernels, on_device(): pl.pallas_call(kernel, out_shape=(out, out, out), in_specs=[pl.BlockSpec(...  26 us
    unnamed x7, local copies, waits for them, and re-layouts  2.77 us

profile of v1, /device:TPU:19, one launch (start us, length us, event | category | flops | bytes accessed | tf_op | source)
XLA Modules:
  0.0 29.4 jit_solution(4321150344782212392)
XLA Ops:
  0.6 26.0 %shard_map.67 = (f32[1,2,16,256]{3,2,1,0:T(8,128)}, f32[1,2,16,256]{3,2,1,0:T(8,128)}, f32[1,2,16,256]{3,2,1,0:T(8,128)}) custom-call(f32[1,2,16,256]{3,2,1,0:T(8,128)} %states.1, s32[64,256]{1,0:T(8,128)} %vel_x.1, s32[64,256]{1,0:T(8,128)} %vel_y.1, s32[64,256]{1,0:T(8,128)} %diffus.1), custom_call_target="tpu_custom_call" | custom-call | tf_op jit(solution)/shard_map/pallas_call | solution.py:300
  26.6 0.0 copy-start.1
  26.6 1.4 %copy.10 = f32[1,2,16,256]{3,2,1,0:T(8,128)} copy(f32[1,2,16,256]{3,2,1,0:T(8,128)} %get-tuple-element.6) | data formatting | bytes 65536
  28.0 0.0 copy-done.1
  28.0 0.0 copy-start
  28.0 0.6 %copy.11 = f32[1,2,16,256]{3,2,1,0:T(8,128)} copy(f32[1,2,16,256]{3,2,1,0:T(8,128)S(1)} %copy-done.1) | data formatting | bytes 65536
  28.6 0.2 copy-done
  28.8 0.6 %copy.12 = f32[1,2,16,256]{3,2,1,0:T(8,128)} copy(f32[1,2,16,256]{3,2,1,0:T(8,128)S(1)} %copy-done) | data formatting | bytes 65536
Async XLA Ops:
  26.6 1.4 %copy-start.1 = (f32[1,2,16,256]{3,2,1,0:T(8,128)S(1)}, f32[1,2,16,256]{3,2,1,0:T(8,128)}, u32[]{:S(2)}) copy-start(f32[1,2,16,256]{3,2,1,0:T(8,128)} %get-tuple-element.7) | copy-start | bytes 98308
  28.0 0.8 %copy-start = (f32[1,2,16,256]{3,2,1,0:T(8,128)S(1)}, f32[1,2,16,256]{3,2,1,0:T(8,128)}, u32[]{:S(2)}) copy-start(f32[1,2,16,256]{3,2,1,0:T(8,128)} %get-tuple-element.8) | copy-start | bytes 98308

commit v2 on v1

--- a/solution.py
+++ b/solution.py
@@ -39,35 +39,70 @@
     return [[f(*values) for values in zip(*rows)] for rows in zip(*fields)]
 
 
+def deal(u):
+    tiles = len(u)
+    lane = lax.broadcasted_iota(jnp.int32, (SUB, LANES), 1)
+    out = []
+    for w in range(tiles):
+        column = tiles * lane + w
+        picks = [jnp.take_along_axis(v, column % LANES, axis=1) for v in u]
+        value = picks[0]
+        for v in range(1, tiles):
+            value = jnp.where(column >= v * LANES, picks[v], value)
+        out.append(value)
+    return out
+
+
+def undeal(u):
+    tiles = len(u)
+    lane = lax.broadcasted_iota(jnp.int32, (SUB, LANES), 1)
+    out = []
+    for v in range(tiles):
+        column = v * LANES + lane
+        picks = [jnp.take_along_axis(x, column // tiles, axis=1) for x in u]
+        value = picks[0]
+        for w in range(1, tiles):
+            value = jnp.where(column % tiles == w, picks[w], value)
+        out.append(value)
+    return out
+
+
 def advance(fields, coefs):
     stacks, tiles = len(fields[0]), len(fields[0][0])
-    lane = lax.broadcasted_iota(jnp.int32, (SUB, LANES), 1)
-    first, last = lane == 0, lane == LANES - 1
     out = [[[None] * tiles for _ in range(stacks)] for _ in fields]
     tops = [[pltpu.roll(u[stacks - 1][w], 1, 0) for w in range(tiles)] for u in fields]
     bottoms = [[pltpu.roll(u[0][w], SUB - 1, 0) for w in range(tiles)] for u in fields]
     for k in range(stacks):
         c = [[coefs[i, k, :, w * LANES : (w + 1) * LANES] for w in range(tiles)] for i in range(5)]
         for f, u in enumerate(fields):
-            right = [pltpu.roll(v, 1, 1) for v in u[k]]
-            left = [pltpu.roll(v, LANES - 1, 1) for v in u[k]]
+            right = pltpu.roll(u[k][tiles - 1], 1, 1)
+            left = pltpu.roll(u[k][0], LANES - 1, 1)
             for w in range(tiles):
                 a = u[k - 1][w] if k else tops[f][w]
                 b = u[k + 1][w] if k + 1 < stacks else bottoms[f][w]
-                l = jnp.where(first, right[w - 1], right[w]) if w else right[w]
-                r = jnp.where(last, left[w + 1], left[w]) if w + 1 < tiles else left[w]
-                out[f][k][w] = (c[0][w] * u[k][w] + (c[1][w] * a + c[2][w] * b)) + (c[3][w] * l + c[4][w] * r)
+                l = u[k][w - 1] if w else right
+                r = u[k][w + 1] if w + 1 < tiles else left
+                near = c[0][w] * u[k][w] + (c[1][w] * a + c[2][w] * b)
+                if w == 0:
+                    out[f][k][w] = (near + c[4][w] * r) + c[3][w] * l
+                else:
+                    out[f][k][w] = (near + c[3][w] * l) + c[4][w] * r
     return out
 
 
-def propagate(fields, coefs, count):
-    return lax.fori_loop(0, count, lambda _, now: advance(now, coefs), fields)
+def propagate(fields, coefs, count, unroll=4):
+    def turn(_, now):
+        for _ in range(unroll):
+            now = advance(now, coefs)
+        return now
+
+    return lax.fori_loop(0, count // unroll, turn, fields)
 
 
 def kernel(
     states, vel_x, vel_y, diffus, corrected, advanced, residual,
-    tables, fine, coarse, gathered, starts, addends, last_residual, blocks, plain,
-    table_sem, send_sem, recv_sem, block_send, block_recv, out_send, out_recv,
+    tables, own_block, staged, fine, coarse, gathered, starts, addends, last_residual, blocks, plain, outgoing,
+    table_sem, own_sem, send_sem, recv_sem, block_send, block_recv, out_send, out_recv,
 ):
     groups, places = lax.axis_size("tm") // 2, lax.axis_size("space")
     p, s = lax.axis_index("tm"), lax.axis_index("space")
@@ -86,6 +121,8 @@
         for i, ref in enumerate((vel_x, vel_y, diffus))
         for w in range(tiles)
     ]
+    own_load = pltpu.make_async_copy(states.at[0], own_block, own_sem)
+    own_load.start()
     for copy in loads:
         copy.start()
 
@@ -112,54 +149,54 @@
 
     lax.fori_loop(0, g, greet_block, 0)
     ahead = groups - 1 - g
+    tracers = states.shape[1]
+    own_load.wait()
+    for t in range(tracers):
+        for i in range(0, rows, SUB):
+            natural = [own_block[t, i : i + SUB, columns(w)] for w in range(tiles)]
+            for w, value in enumerate(deal(natural)):
+                staged[t, w, i : i + SUB] = value
+
     more = jnp.where(ahead > 0, 2 * places, 0)
     pl.semaphore_wait(barrier, (1 - x) * (2 * places - 1) + more + ahead + 1)
 
     my_rows = pl.ds(pl.multiple_of(s * rows, SUB), rows)
-    partner_rows = pl.ds(pl.multiple_of(partner * rows, SUB), rows)
-
-    def piece(role, pp, ss, slot, w):
+
+    def piece(role, pp, ss, slot):
         return pltpu.make_async_remote_copy(
-            src_ref=states.at[0, ss % 2, :, columns(w)],
-            dst_ref=gathered.at[role, w, my_rows],
-            send_sem=send_sem.at[slot, w],
+            src_ref=staged.at[ss % 2],
+            dst_ref=gathered.at[role, :, my_rows],
+            send_sem=send_sem.at[slot],
             recv_sem=recv_sem.at[role],
             device_id=(pp, ss),
             device_id_type=MESH,
         )
 
-    own = [
-        pltpu.make_async_copy(states.at[0, tracer, :, columns(w)], gathered.at[2, w, my_rows], recv_sem.at[2])
-        for w in range(tiles)
-    ]
+    own = pltpu.make_async_copy(staged.at[tracer], gathered.at[2, :, my_rows], recv_sem.at[2])
 
     def to_next(act):
         @pl.when(ahead > 0)
         def _():
             for m in range(2):
                 for ss in range(places):
-                    for w in range(tiles):
-                        act(piece(x, 2 * g + 2 + m, ss, m * places + ss, w))
+                    act(piece(x, 2 * g + 2 + m, ss, m * places + ss))
 
     def to_group(act):
         @pl.when(x == 0)
         def _():
             for ss in range(places):
-                for w in range(tiles):
-                    act(piece(2, 2 * g + 1, ss, 3 * places + ss, w))
+                act(piece(2, 2 * g + 1, ss, 3 * places + ss))
             for ss in range(places):
                 @pl.when(s != ss)
                 def _():
-                    for w in range(tiles):
-                        act(piece(2, 2 * g, ss, 2 * places + ss, w))
+                    act(piece(2, 2 * g, ss, 2 * places + ss))
 
     to_next(lambda copy: copy.start())
     to_group(lambda copy: copy.start())
 
     @pl.when(x == 0)
     def _():
-        for copy in own:
-            copy.start()
+        own.start()
 
     @pl.when(g == 0)
     def _():
@@ -171,8 +208,7 @@
     scale = jnp.where(tracer == 0, 1.0, 0.5).astype(jnp.float32)
     sub = lax.broadcasted_iota(jnp.int32, (SUB, LANES), 0)
     lane = lax.broadcasted_iota(jnp.int32, (SUB, LANES), 1)
-    for k, w in [(k, w) for k in range(stacks) for w in range(tiles)]:
-        cx, cy, d = (tables[i, w, pl.ds(k, SUB, stride=stacks), :].astype(jnp.float32) for i in range(3))
+    def put_coefficients(k, w, cx, cy, d):
         cx, cy, d = 0.01 * cx, 0.01 * cy, (0.005 * d) * scale
         above, below = d + jnp.maximum(cx, 0.0), d - jnp.minimum(cx, 0.0)
         before, after = d + jnp.maximum(cy, 0.0), d - jnp.minimum(cy, 0.0)
@@ -190,30 +226,40 @@
             for i, value in enumerate((above, below, before, after)):
                 table[i + 1, k, :, columns(w)] = factor * value
 
+    for k in range(stacks):
+        dealt = []
+        for i in range(3):
+            levels = [tables[i, w, pl.ds(k, SUB, stride=stacks), :].astype(jnp.float32) for w in range(tiles)]
+            dealt.append(deal(levels))
+        for w in range(tiles):
+            put_coefficients(k, w, *(table[w] for table in dealt))
+
     def arrive(role):
         pltpu.make_async_remote_copy(
             src_ref=gathered.at[role],
             dst_ref=gathered.at[role],
-            send_sem=send_sem.at[0, 0],
+            send_sem=send_sem.at[0],
             recv_sem=recv_sem.at[role],
             device_id=(p, partner),
             device_id_type=MESH,
         ).wait_recv()
 
     arrive(2)
+    first = load_rows(gathered.at[2], stacks, tiles)
+    (d1,) = propagate([first], fine, STEPS)
+    store(starts.at[1], d1)
 
     @pl.when(g > 0)
     def _():
         arrive(0)
         arrive(1)
 
-    a0, b0, d0 = (load_rows(gathered.at[role], stacks, tiles) for role in range(3))
-    a1, b1, d1 = propagate([a0, b0, d0], fine, STEPS)
+    a0, b0 = (load_rows(gathered.at[role], stacks, tiles) for role in range(2))
+    a1, b1 = propagate([a0, b0], fine, STEPS, 1)
     at_start = g == 0
     b1 = each(lambda u, v: jnp.where(at_start, v, u), b1, load_rows(gathered.at[2], stacks, tiles))
     store(starts.at[0], b1)
-    store(starts.at[1], d1)
-    a2, b2 = propagate([a1, b1], fine, STEPS)
+    a2, b2 = propagate([a1, b1], fine, STEPS, 1)
     r0 = each(lambda u, v: jnp.where(at_start, 0.0, u - v), a2, load(starts.at[0], stacks, tiles))
     store(addends.at[0], r0)
     r1 = each(lambda u, v: u - v, b2, load(starts.at[1], stacks, tiles))
@@ -237,22 +283,28 @@
 
     lax.fori_loop(0, ahead, start_block, 0)
 
-    def hand_over(which, out, w):
+    def hand_over(which, out):
         return pltpu.make_async_remote_copy(
-            src_ref=plain.at[which, w, partner_rows],
-            dst_ref=out.at[0, tracer, :, columns(w)],
-            send_sem=out_send.at[which, w],
-            recv_sem=out_recv.at[which, w],
+            src_ref=outgoing.at[which],
+            dst_ref=out.at[0, tracer],
+            send_sem=out_send.at[which],
+            recv_sem=out_recv.at[which],
             device_id=(p, partner),
             device_id_type=MESH,
         )
 
     def put(which, out, u):
         store_rows(plain.at[which], u)
-        for w in range(tiles):
-            hand_over(which, out, w).start()
-        for w in range(tiles):
-            out[0, tracer, :, columns(w)] = plain[which, w, my_rows]
+        for place, mine in ((partner, False), (s, True)):
+            for i in range(0, rows, SUB):
+                at = pl.ds(pl.multiple_of(place * rows + i, SUB), SUB)
+                for w, value in enumerate(undeal([plain[which, w, at] for w in range(tiles)])):
+                    if mine:
+                        out[0, tracer, i : i + SUB, columns(w)] = value
+                    else:
+                        outgoing[which, i : i + SUB, columns(w)] = value
+            if not mine:
+                hand_over(which, out).start()
 
     put(0, residual, each(lambda u, v: jnp.where(x == 0, u, v), load(addends.at[0], stacks, tiles), load(last_residual, stacks, tiles)))
 
@@ -286,8 +338,7 @@
 
     lax.fori_loop(0, ahead, end_block, 0)
     for which, out in enumerate((residual, corrected, advanced)):
-        for w in range(tiles):
-            hand_over(which, out, w).wait()
+        hand_over(which, out).wait()
 
 
 def on_device(states, vel_x, vel_y, diffus):
@@ -304,6 +355,8 @@
         out_specs=(pl.BlockSpec(memory_space=pltpu.VMEM),) * 3,
         scratch_shapes=[
             pltpu.VMEM((3, *grid), jnp.int32),
+            pltpu.VMEM(states.shape[1:], jnp.float32),
+            pltpu.VMEM((states.shape[1], tiles, states.shape[2], LANES), jnp.float32),
             pltpu.VMEM((5, *field), jnp.float32),
             pltpu.VMEM((5, *field), jnp.float32),
             pltpu.VMEM((3, *grid), jnp.float32),
@@ -312,13 +365,15 @@
             pltpu.VMEM(field, jnp.float32),
             pltpu.VMEM((groups, *field), jnp.float32),
             pltpu.VMEM((3, *grid), jnp.float32),
+            pltpu.VMEM((3, *states.shape[2:]), jnp.float32),
             pltpu.SemaphoreType.DMA((3, tiles)),
-            pltpu.SemaphoreType.DMA((4 * places, tiles)),
+            pltpu.SemaphoreType.DMA(()),
+            pltpu.SemaphoreType.DMA((4 * places,)),
             pltpu.SemaphoreType.DMA((3,)),
             pltpu.SemaphoreType.DMA((groups,)),
             pltpu.SemaphoreType.DMA((groups,)),
-            pltpu.SemaphoreType.DMA((3, tiles)),
-            pltpu.SemaphoreType.DMA((3, tiles)),
+            pltpu.SemaphoreType.DMA((3,)),
+            pltpu.SemaphoreType.DMA((3,)),
         ],
         compiler_params=pltpu.CompilerParams(collective_id=0, has_side_effects=True),
     )(states, vel_x, vel_y, diffus)

time: 29.9 us -> 27.7 us (0.926)
  Pallas kernels: 26 us -> 24 us
    pallas_call x1, Pallas kernels: 26 us -> 24 us  [on_device(): pl.pallas_call(kernel, out_shape=(out, out, out), in_specs=[pl.BlockSpec(...]
where the time goes in v2:
time: 27.7 us; the launch traced here: 27.4 us
  Pallas kernels  24 us (87%)
  local copies, waits for them, and re-layouts  2.77 us (10%)
  between operations  0.65 us (2%)
    pallas_call x1, Pallas kernels, on_device(): pl.pallas_call(kernel, out_shape=(out, out, out), in_specs=[pl.BlockSpec(...  24 us
    unnamed x7, local copies, waits for them, and re-layouts  2.77 us

profile of v2, /device:TPU:19, one launch (start us, length us, event | category | flops | bytes accessed | tf_op | source)
XLA Modules:
  0.0 27.4 jit_solution(3958958139418315106)
XLA Ops:
  0.6 24.0 %shard_map.67 = (f32[1,2,16,256]{3,2,1,0:T(8,128)}, f32[1,2,16,256]{3,2,1,0:T(8,128)}, f32[1,2,16,256]{3,2,1,0:T(8,128)}) custom-call(f32[1,2,16,256]{3,2,1,0:T(8,128)} %states.1, s32[64,256]{1,0:T(8,128)} %vel_x.1, s32[64,256]{1,0:T(8,128)} %vel_y.1, s32[64,256]{1,0:T(8,128)} %diffus.1), custom_call_target="tpu_custom_call" | custom-call | tf_op jit(solution)/shard_map/pallas_call | solution.py:351
  24.6 0.0 copy-start.1
  24.6 1.4 %copy.10 = f32[1,2,16,256]{3,2,1,0:T(8,128)} copy(f32[1,2,16,256]{3,2,1,0:T(8,128)} %get-tuple-element.6) | data formatting | bytes 65536
  26.0 0.0 copy-done.1
  26.0 0.0 copy-start
  26.0 0.6 %copy.11 = f32[1,2,16,256]{3,2,1,0:T(8,128)} copy(f32[1,2,16,256]{3,2,1,0:T(8,128)S(1)} %copy-done.1) | data formatting | bytes 65536
  26.6 0.2 copy-done
  26.8 0.6 %copy.12 = f32[1,2,16,256]{3,2,1,0:T(8,128)} copy(f32[1,2,16,256]{3,2,1,0:T(8,128)S(1)} %copy-done) | data formatting | bytes 65536
Async XLA Ops:
  24.6 1.4 %copy-start.1 = (f32[1,2,16,256]{3,2,1,0:T(8,128)S(1)}, f32[1,2,16,256]{3,2,1,0:T(8,128)}, u32[]{:S(2)}) copy-start(f32[1,2,16,256]{3,2,1,0:T(8,128)} %get-tuple-element.7) | copy-start | bytes 98308
  26.0 0.8 %copy-start = (f32[1,2,16,256]{3,2,1,0:T(8,128)S(1)}, f32[1,2,16,256]{3,2,1,0:T(8,128)}, u32[]{:S(2)}) copy-start(f32[1,2,16,256]{3,2,1,0:T(8,128)} %get-tuple-element.8) | copy-start | bytes 98308
